TPU v7x, 32 devices: a whole 2x2x4 slice. The times are simulated.
32 devices in a mesh: pty: 16 (over z, y, core), tx: 2 (over x).
Axes of the slice: x: 2, y: 2, z: 4, core: 2. Of those that a mesh axis runs over, the one named last changes fastest.
Arguments:
- state: float32 [5, 384, 64, 128], P(None, 'pty', 'tx'), may hold values from -6 to 6
- sound_speed_sq: float32 [384, 64, 128], P('pty', 'tx'), may hold values from 0.05 to 0.3
- buoyancy_freq_sq: float32 [128], replicated, may hold values from 0.2 to 2
- adjacency: int32 [6, 4, 3], replicated, may hold values from 0 to 5, as said below
Outputs:
- advanced: float32 [5, 384, 64, 128], P(None, 'pty', 'tx')
Inputs may be any that keep to these rules, and one draw needn't show every extreme that they name: adjacency[k, e] = (q, f, r): edge e of panel k touches edge f of panel q, position s meeting position s of f if r = 0 and 63 - s if r = 1; the relation is symmetric, q differs from k, and the six panels with their edges close into a cube.
All inputs are finite; a program needn't handle non-finite values.
Results may differ from a plain program's by a relative error of at most 0.00002.
Values sent between devices are 32-bit elements; how exact they have to be, the bound alone decides.
A program may use at most 64 MiB of HBM per device.

v0:
```python
import jax
import jax.numpy as jnp
from jax import lax
from jax.sharding import PartitionSpec as P

STEP = 0.5


def padded(x, sides, width):
    for axis, dim in sides:
        size, length = (lax.axis_size(axis), x.shape[dim])
        up = [(i, (i + 1) % size) for i in range(size)]
        down = [(j, i) for i, j in up]
        last = lax.slice_in_dim(x, length - width, length, axis=dim)
        initial = lax.slice_in_dim(x, 0, width, axis=dim)
        before = lax.ppermute(last, axis, up)
        after = lax.ppermute(initial, axis, down)
        x = jnp.concatenate([before, x, after], axis=dim)
    return x


def level_diff(values):
    lowest = values[..., 1:2] - values[..., 0:1]
    middle = 0.5 * (values[..., 2:] - values[..., :-2])
    highest = values[..., -1:] - values[..., -2:-1]
    return jnp.concatenate([lowest, middle, highest], axis=-1)


def wall_diff(values):
    lowest = values[..., 1:2] + values[..., 0:1]
    middle = 0.5 * (values[..., 2:] - values[..., :-2])
    highest = -(values[..., -1:] + values[..., -2:-1])
    return jnp.concatenate([lowest, middle, highest], axis=-1)


def locate(pty_dest, tx_dest, tile_rows, tile_cols, panel_side, tx_count, adjacency, offset_rows):
    rows_all = 6 * panel_side
    row_index = jnp.arange(tile_rows, dtype=jnp.int32)[None, :]
    col_index = jnp.arange(tile_cols, dtype=jnp.int32)[None, :]
    row_base = pty_dest * tile_rows
    global_row = row_base + row_index
    unrolled = (global_row + rows_all - offset_rows) % rows_all
    shape_rows = global_row.shape
    at_west = tx_dest == 0
    at_east = tx_dest == tx_count - 1
    col_valid = jnp.broadcast_to(at_west | at_east, shape_rows)
    col_panel = unrolled // panel_side
    col_place = unrolled % panel_side
    col_edge = jnp.broadcast_to(jnp.where(at_west, 3, 1).astype(jnp.int32), shape_rows)
    offset = (row_base + rows_all - offset_rows) % panel_side
    start_row = (panel_side - offset) % panel_side
    end_row = (panel_side - 1 - offset) % panel_side
    along = tx_dest * tile_cols + col_index
    shape_cols = along.shape
    start_valid = jnp.broadcast_to(start_row < tile_rows, shape_cols)
    end_valid = jnp.broadcast_to(end_row < tile_rows, shape_cols)
    start_panel = jnp.broadcast_to(
        (row_base + start_row + rows_all - offset_rows) % rows_all // panel_side, shape_cols
    )
    end_panel = jnp.broadcast_to(
        (row_base + end_row + rows_all - offset_rows) % rows_all // panel_side, shape_cols
    )
    valid = jnp.concatenate([col_valid, start_valid, end_valid], axis=1)
    panel_id = jnp.concatenate([col_panel, start_panel, end_panel], axis=1)
    edge_id = jnp.concatenate(
        [col_edge, jnp.zeros(shape_cols, jnp.int32), jnp.full(shape_cols, 2, jnp.int32)], axis=1
    )
    place = jnp.concatenate([col_place, along, along], axis=1)
    edge_key = panel_id * 4 + edge_id
    matches = edge_key[..., None] == jnp.arange(24, dtype=jnp.int32)
    flat_table = adjacency.reshape(24, 3)
    other_panel = jnp.sum(jnp.where(matches, flat_table[:, 0], 0), axis=-1)
    other_edge = jnp.sum(jnp.where(matches, flat_table[:, 1], 0), axis=-1)
    reversal = jnp.sum(jnp.where(matches, flat_table[:, 2], 0), axis=-1)
    other_place = jnp.where(reversal == 1, panel_side - 1 - place, place)
    on_column = (other_edge == 1) | (other_edge == 3)
    source_unrolled = other_panel * panel_side + jnp.where(
        on_column, other_place, jnp.where(other_edge == 0, 0, panel_side - 1)
    )
    source_row = (source_unrolled + offset_rows) % rows_all
    source_pty = source_row // tile_rows
    source_slot = jnp.where(
        on_column,
        source_row % tile_rows,
        tile_rows + jnp.where(other_edge == 0, 0, tile_cols) + other_place % tile_cols,
    )
    source_tx = jnp.where(
        on_column, jnp.where(other_edge == 3, 0, tx_count - 1), other_place // tile_cols
    )
    boundary = other_panel * 2 + jnp.where(other_edge == 2, 1, 0)
    compact_slot = jnp.where(
        on_column, source_row, 6 * panel_side + boundary * tile_cols + other_place % tile_cols
    )
    return (valid, source_pty, source_tx, source_slot, compact_slot)


def tendency(fields, speed_sq, freq_sq, adjacency, pty_here, tx_here):
    tx_count = lax.axis_size("tx")
    pty_count = lax.axis_size("pty")
    tile_rows = fields.shape[1]
    tile_cols = fields.shape[2]
    levels = fields.shape[3]
    panel_side = tile_cols * tx_count
    rows_all = 6 * panel_side
    offset_rows = tile_rows // 2
    point_count = tile_rows + 2 * tile_cols
    vel_u, vel_v, vel_w, pressure, buoyancy = (
        fields[0],
        fields[1],
        fields[2],
        fields[3],
        fields[4],
    )
    horizontal = jnp.stack([vel_u, vel_v, pressure])
    extended = padded(horizontal, (("pty", 1), ("tx", 2)), 1)
    row_place = (
        pty_here * tile_rows + jnp.arange(tile_rows, dtype=jnp.int32) + rows_all - offset_rows
    ) % panel_side
    col_place = tx_here * tile_cols + jnp.arange(tile_cols, dtype=jnp.int32)
    row_after = extended[0:3:2, 2:, 1:-1]
    row_before = extended[0:3:2, :-2, 1:-1]
    row_here = horizontal[0:3:2]
    row_start = (row_place == 0)[None, :, None, None]
    row_end = (row_place == panel_side - 1)[None, :, None, None]
    along_rows = jnp.where(
        row_start,
        row_after - row_here,
        jnp.where(row_end, row_here - row_before, 0.5 * (row_after - row_before)),
    )
    col_after = extended[1:, 1:-1, 2:]
    col_before = extended[1:, 1:-1, :-2]
    col_here = horizontal[1:]
    col_start = (col_place == 0)[None, None, :, None]
    col_end = (col_place == panel_side - 1)[None, None, :, None]
    along_cols = jnp.where(
        col_start,
        col_after - col_here,
        jnp.where(col_end, col_here - col_before, 0.5 * (col_after - col_before)),
    )
    tend_u = -along_rows[1]
    tend_v = -along_cols[1]
    tend_w = -level_diff(pressure) + buoyancy
    tend_b = -freq_sq * vel_w
    tend_p = -speed_sq * (along_rows[0] + along_cols[0] + wall_diff(vel_w))
    row_base = pty_here * tile_rows
    offset = (row_base + rows_all - offset_rows) % panel_side
    start_row = (panel_side - offset) % panel_side
    end_row = (panel_side - 1 - offset) % panel_side
    start_take = jnp.minimum(start_row, tile_rows - 1)
    end_take = jnp.minimum(end_row, tile_rows - 1)
    at_west = tx_here == 0
    col_take = jnp.where(at_west, 0, tile_cols - 1).astype(jnp.int32)
    col_sign = jnp.where(at_west, -1.0, 1.0).astype(jnp.float32)
    start_p = lax.dynamic_index_in_dim(pressure, start_take, 0, keepdims=False)
    start_n = -lax.dynamic_index_in_dim(vel_u, start_take, 0, keepdims=False)
    end_p = lax.dynamic_index_in_dim(pressure, end_take, 0, keepdims=False)
    end_n = lax.dynamic_index_in_dim(vel_u, end_take, 0, keepdims=False)
    col_p = lax.dynamic_index_in_dim(pressure, col_take, 1, keepdims=False)
    col_n = col_sign * lax.dynamic_index_in_dim(vel_v, col_take, 1, keepdims=False)
    own_pack = jnp.stack(
        [
            jnp.concatenate([col_p, start_p, end_p], axis=0),
            jnp.concatenate([col_n, start_n, end_n], axis=0),
        ],
        axis=1,
    )
    own_valid = locate(
        jnp.reshape(pty_here, (1, 1)),
        jnp.reshape(tx_here, (1, 1)),
        tile_rows,
        tile_cols,
        panel_side,
        tx_count,
        adjacency,
        offset_rows,
    )[0][0]
    gathered = lax.all_gather(own_pack[None], "pty", axis=0, tiled=True)
    flat_pack = gathered.reshape(pty_count * point_count, 2, levels)
    tx_dest = jnp.arange(tx_count, dtype=jnp.int32)[:, None]
    pty_dest = jnp.full((tx_count, 1), pty_here, jnp.int32)
    valid, source_pty, source_tx, source_slot, compact_slot = locate(
        pty_dest, tx_dest, tile_rows, tile_cols, panel_side, tx_count, adjacency, offset_rows
    )
    taken = valid & (source_tx == tx_here)
    picks = jnp.where(taken, source_pty * point_count + source_slot, 0).reshape(-1)
    outgoing = (
        jnp.take(flat_pack, picks, axis=0) * taken.reshape(-1).astype(jnp.float32)[:, None, None]
    )
    received = lax.psum_scatter(outgoing, "tx", scatter_dimension=0, tiled=True)
    weight_valid = own_valid.astype(jnp.float32)[:, None]
    sat_p = (own_pack[:, 1] + received[:, 1]) * weight_valid
    sat_n = (own_pack[:, 0] - received[:, 0]) * weight_valid
    col_sat_p = sat_p[:tile_rows]
    start_sat_p = sat_p[tile_rows : tile_rows + tile_cols]
    end_sat_p = sat_p[tile_rows + tile_cols :]
    col_sat_n = sat_n[:tile_rows]
    start_sat_n = sat_n[tile_rows : tile_rows + tile_cols]
    end_sat_n = sat_n[tile_rows + tile_cols :]
    col_mask = (jnp.arange(tile_cols, dtype=jnp.int32) == col_take).astype(jnp.float32)[
        None, :, None
    ]
    start_mask = (jnp.arange(tile_rows, dtype=jnp.int32) == start_row).astype(jnp.float32)[
        :, None, None
    ]
    end_mask = (jnp.arange(tile_rows, dtype=jnp.int32) == end_row).astype(jnp.float32)[
        :, None, None
    ]
    tend_p = tend_p + speed_sq * (
        col_mask * col_sat_p[:, None, :]
        + start_mask * start_sat_p[None]
        + end_mask * end_sat_p[None]
    )
    tend_u = tend_u - start_mask * start_sat_n[None] + end_mask * end_sat_n[None]
    tend_v = tend_v + col_mask * (col_sign * col_sat_n)[:, None, :]
    return jnp.stack([tend_u, tend_v, tend_w, tend_p, tend_b])


def on_device(state, sound_speed_sq, buoyancy_freq_sq, adjacency):
    pty_here = lax.axis_index("pty")
    tx_here = lax.axis_index("tx")
    section_one = state + STEP * tendency(
        state, sound_speed_sq, buoyancy_freq_sq, adjacency, pty_here, tx_here
    )
    section_two = 0.75 * state + 0.25 * (
        section_one
        + STEP
        * tendency(section_one, sound_speed_sq, buoyancy_freq_sq, adjacency, pty_here, tx_here)
    )
    return 1.0 / 3.0 * state + 2.0 / 3.0 * (
        section_two
        + STEP
        * tendency(section_two, sound_speed_sq, buoyancy_freq_sq, adjacency, pty_here, tx_here)
    )


def solution(mesh):
    in_specs = (P(None, "pty", "tx", None), P("pty", "tx", None), P(), P())
    out_specs = P(None, "pty", "tx", None)
    return jax.shard_map(
        on_device, mesh=mesh, in_specs=in_specs, out_specs=out_specs, check_vma=False
    )
```

profile of v0, /device:TPU:0, one launch (start us, length us, event | category | flops | bytes accessed | tf_op | source)
XLA Modules:
  0.0 266.2 jit_solution(6213916676011198944)
XLA Ops:
  6.5 2.7 %copy.226 = f32[5,24,32,128]{3,1,2,0:T(8,128)S(1)} copy(f32[5,24,32,128]{3,2,1,0:T(8,128)} %param.6) | data formatting | bytes 3932160 | tf_op args[0]
  14.6 5.0 %collective-permute-start.1 = (f32[3,1,32,128]{3,1,2,0:T(1,128)}, f32[3,1,32,128]{3,1,2,0:T(1,128)}, u32[]{:S(2)}, u32[]{:S(2)}) collective-permute-start(f32[3,1,32,128]{3,1,2,0:T(1,128)} %get-tuple-element.39), channel_id=1, source_target_pairs={{2,0},{4,2},{6,4},{8,6},{10,8},{12,10},{14,12},{16,14},{18,16},{20... | collective-permute-start | bytes 147464 | tf_op jit(solution)/shard_map/ppermute | solution.py:17
  57.6 1.8 copy.234
  60.3 1.8 copy.235
  62.1 1.7 copy.237
  68.9 1.9 collective-permute-start.2
  72.1 3.0 %gather_fusion = f32[176,2,128]{2,1,0:T(2,128)} fusion(f32[1408,2,128]{2,1,0:T(2,128)} %all-gather.7.cloned.1.call-done, s32[1024]{0:T(1024)} %pad_clamp_fusion), kind=kCustom, calls=%fused_computation.clone | custom fusion | bytes 361152 | tf_op jit(solution)/shard_map/jit(_take)/gather | solution.py:187
  75.1 2.0 select_multiply_fusion.2
  77.2 2.0 select_select_fusion.4
  79.2 19.2 %all-reduce.7.cloned.1.call-done = f32[176,2,128]{2,1,0:T(2,128)} async-done(((f32[176,2,128]{2,1,0:T(2,128)}), f32[176,2,128]{2,1,0:T(2,128)}) %all-reduce.7.cloned.1.call-update) | async-done | bytes 180240
  110.5 1.7 fusion.53
  112.2 4.4 %collective-permute-start.5 = (f32[3,1,32,128]{3,1,2,0:T(1,128)}, f32[3,1,32,128]{3,1,2,0:T(1,128)}, u32[]{:S(2)}, u32[]{:S(2)}) collective-permute-start(f32[3,1,32,128]{3,1,2,0:T(1,128)} %get-tuple-element.37), channel_id=1, source_target_pairs={{2,0},{4,2},{6,4},{8,6},{10,8},{12,10},{14,12},{16,14},{18,16},{20... | collective-permute-start | bytes 147464 | tf_op jit(solution)/shard_map/ppermute | solution.py:17
  122.2 1.8 copy.247
  124.1 1.7 copy.249
  126.6 1.7 copy.250
  130.4 1.8 collective-permute-start.7
  133.4 15.3 %all-gather.9.cloned.1.call-done = f32[1408,2,128]{2,1,0:T(2,128)} async-done(((f32[88,2,128]{2,1,0:T(2,128)}), f32[1408,2,128]{2,1,0:T(2,128)}) %all-gather.9.cloned.1.call-update) | async-done | bytes 1441808 | tf_op jit(solution)/shard_map/all_gather | solution.py:177
  148.7 2.3 gather_fusion.1
  152.3 2.0 select_select_fusion.2
  154.3 19.0 %all-reduce.9.cloned.1.call-done = f32[176,2,128]{2,1,0:T(2,128)} async-done(((f32[176,2,128]{2,1,0:T(2,128)}), f32[176,2,128]{2,1,0:T(2,128)}) %all-reduce.9.cloned.1.call-update) | async-done | bytes 180240
  180.7 1.7 multiply_add_fusion.1
  185.6 1.7 fusion.51
  187.3 4.4 %collective-permute-start.9 = (f32[3,1,32,128]{3,1,2,0:T(1,128)}, f32[3,1,32,128]{3,1,2,0:T(1,128)}, u32[]{:S(2)}, u32[]{:S(2)}) collective-permute-start(f32[3,1,32,128]{3,1,2,0:T(1,128)} %get-tuple-element.35), channel_id=1, source_target_pairs={{2,0},{4,2},{6,4},{8,6},{10,8},{12,10},{14,12},{16,14},{18,16},{20... | collective-permute-start | bytes 147464 | tf_op jit(solution)/shard_map/ppermute | solution.py:17
  197.3 1.8 copy.255
  199.1 1.7 copy.257
  201.5 1.7 copy.258
  204.7 1.8 collective-permute-start.11
  207.7 16.1 %all-gather.11.cloned.1.call-done = f32[1408,2,128]{2,1,0:T(2,128)} async-done(((f32[88,2,128]{2,1,0:T(2,128)}), f32[1408,2,128]{2,1,0:T(2,128)}) %all-gather.11.cloned.1.call-update) | async-done | bytes 1441808 | tf_op jit(solution)/shard_map/all_gather | solution.py:177
  223.8 2.3 gather_fusion.2
  228.0 2.0 select_select_fusion
  230.0 18.4 %all-reduce.11.cloned.1.call-done = f32[176,2,128]{2,1,0:T(2,128)} async-done(((f32[176,2,128]{2,1,0:T(2,128)}), f32[176,2,128]{2,1,0:T(2,128)}) %all-reduce.11.cloned.1.call-update) | async-done | bytes 180240
  257.7 1.6 copy.261
  (323 shorter events, 102.6 us)
Async XLA Ops:
  6.5 65.5 %all-gather.7.cloned.1.call-start = ((), (), s32[]{:S(2)}) async-start(), calls=%async_computation | async-start | bytes 1531904 | tf_op jit(solution)/shard_map/all_gather | solution.py:177
  9.2 93.4 %copy-start.4 = (f32[5,24,32,128]{3,1,2,0:T(8,128)}, f32[5,24,32,128]{3,1,2,0:T(8,128)S(1)}, u32[]{:S(2)}) copy-start(f32[5,24,32,128]{3,1,2,0:T(8,128)S(1)} %copy.226) | copy-start | bytes 5898244
  13.3 85.1 %all-reduce.7.cloned.1.call-start = ((), (), s32[]{:S(2)}) async-start(), calls=%async_computation.3 | async-start | bytes 360448
  14.2 52.8 %collective-permute-start = (f32[3,1,32,128]{3,1,2,0:T(1,128)}, f32[3,1,32,128]{3,1,2,0:T(1,128)}, u32[]{:S(2)}, u32[]{:S(2)}) collective-permute-start(f32[3,1,32,128]{3,1,2,0:T(1,128)} %get-tuple-element.38), channel_id=1, source_target_pairs={{0,2},{2,4},{4,6},{6,8},{8,10},{10,12},{12,14},{14,16},{16,18},{18... | collective-permute-start | bytes 147464 | tf_op jit(solution)/shard_map/ppermute | solution.py:16
  14.6 52.4 %collective-permute-start.1 = (f32[3,1,32,128]{3,1,2,0:T(1,128)}, f32[3,1,32,128]{3,1,2,0:T(1,128)}, u32[]{:S(2)}, u32[]{:S(2)}) collective-permute-start(f32[3,1,32,128]{3,1,2,0:T(1,128)} %get-tuple-element.39), channel_id=1, source_target_pairs={{2,0},{4,2},{6,4},{8,6},{10,8},{12,10},{14,12},{16,14},{18,16},{20... | collective-permute-start | bytes 147464 | tf_op jit(solution)/shard_map/ppermute | solution.py:17
  68.9 8.3 %collective-permute-start.2 = (f32[3,26,1,128]{3,1,2,0:T(8,128)}, f32[3,26,1,128]{3,1,2,0:T(8,128)}, u32[]{:S(2)}, u32[]{:S(2)}) collective-permute-start(f32[3,26,1,128]{3,1,2,0:T(8,128)} %get-tuple-element.32), channel_id=1, source_target_pairs={{1,0},{0,1},{3,2},{2,3},{5,4},{4,5},{7,6},{6,7},{9,8},{8,9},{11,10... | collective-permute-start | bytes 119816 | tf_op jit(solution)/shard_map/ppermute | solution.py:17
  70.8 6.4 %collective-permute-start.3 = (f32[3,26,1,128]{3,1,2,0:T(8,128)}, f32[3,26,1,128]{3,1,2,0:T(8,128)}, u32[]{:S(2)}, u32[]{:S(2)}) collective-permute-start(f32[3,26,1,128]{3,1,2,0:T(8,128)} %get-tuple-element.33), channel_id=1, source_target_pairs={{0,1},{1,0},{2,3},{3,2},{4,5},{5,4},{6,7},{7,6},{8,9},{9,8},{10,11... | collective-permute-start | bytes 119816 | tf_op jit(solution)/shard_map/ppermute | solution.py:16
  77.1 71.6 %all-gather.9.cloned.1.call-start = ((), (), s32[]{:S(2)}) async-start(), calls=%async_computation.1 | async-start | bytes 1531904 | tf_op jit(solution)/shard_map/all_gather | solution.py:177
  79.2 23.4 %copy-start.30 = (f32[1,24,32,1]{3,1,2,0:T(8,128)S(1)}, f32[1,24,32,1]{3,1,2,0:T(8,128)}, u32[]{:S(2)}) copy-start(f32[1,24,32,1]{3,1,2,0:T(8,128)} %copy.237) | copy-start | bytes 9220
  79.2 23.4 %copy-start.33 = (f32[1,24,32,126]{3,1,2,0:T(8,128)S(1)}, f32[1,24,32,126]{3,1,2,0:T(8,128)}, u32[]{:S(2)}) copy-start(f32[1,24,32,126]{3,1,2,0:T(8,128)} %fusion.45) | copy-start | bytes 1161220
  109.3 64.0 %all-reduce.9.cloned.1.call-start = ((), (), s32[]{:S(2)}) async-start(), calls=%async_computation.4 | async-start | bytes 360448
  112.2 16.1 %collective-permute-start.4 = (f32[3,1,32,128]{3,1,2,0:T(1,128)}, f32[3,1,32,128]{3,1,2,0:T(1,128)}, u32[]{:S(2)}, u32[]{:S(2)}) collective-permute-start(f32[3,1,32,128]{3,1,2,0:T(1,128)} %get-tuple-element.36), channel_id=1, source_target_pairs={{0,2},{2,4},{4,6},{6,8},{8,10},{10,12},{12,14},{14,16},{16,18},{18... | collective-permute-start | bytes 147464 | tf_op jit(solution)/shard_map/ppermute | solution.py:16
  112.2 16.1 %collective-permute-start.5 = (f32[3,1,32,128]{3,1,2,0:T(1,128)}, f32[3,1,32,128]{3,1,2,0:T(1,128)}, u32[]{:S(2)}, u32[]{:S(2)}) collective-permute-start(f32[3,1,32,128]{3,1,2,0:T(1,128)} %get-tuple-element.37), channel_id=1, source_target_pairs={{2,0},{4,2},{6,4},{8,6},{10,8},{12,10},{14,12},{16,14},{18,16},{20... | collective-permute-start | bytes 147464 | tf_op jit(solution)/shard_map/ppermute | solution.py:17
  121.1 7.2 %copy-start.10 = (f32[1,24,32,128]{3,1,2,0:T(8,128)S(1)}, f32[1,24,32,128]{3,1,2,0:T(8,128)}, u32[]{:S(2)}) copy-start(f32[1,24,32,128]{3,1,2,0:T(8,128)} %copy-done.8) | copy-start | bytes 1179652
  126.6 5.6 %copy-start.66 = (pred[24]{0:T(512)(128)(4,1)S(1)}, pred[24]{0:T(512)(128)(4,1)}, u32[]{:S(2)}) copy-start(pred[24]{0:T(512)(128)(4,1)} %get-tuple-element.101) | copy-start | bytes 76
  129.5 21.6 %copy-start.58 = (f32[176]{0:T(256)S(1)}, f32[176]{0:T(256)}, u32[]{:S(2)}) copy-start(f32[176]{0:T(256)} %get-tuple-element.9) | copy-start | bytes 2116
  129.5 21.6 %copy-start.60 = (pred[176]{0:T(512)(128)(4,1)S(1)}, pred[176]{0:T(512)(128)(4,1)}, u32[]{:S(2)}) copy-start(pred[176]{0:T(512)(128)(4,1)} %get-tuple-element.11) | copy-start | bytes 532
  130.2 22.1 %collective-permute-start.6 = (f32[3,26,1,128]{3,1,2,0:T(8,128)}, f32[3,26,1,128]{3,1,2,0:T(8,128)}, u32[]{:S(2)}, u32[]{:S(2)}) collective-permute-start(f32[3,26,1,128]{3,1,2,0:T(8,128)} %get-tuple-element.30), channel_id=1, source_target_pairs={{1,0},{0,1},{3,2},{2,3},{5,4},{4,5},{7,6},{6,7},{9,8},{8,9},{11,10... | collective-permute-start | bytes 119816 | tf_op jit(solution)/shard_map/ppermute | solution.py:17
  130.4 22.0 %collective-permute-start.7 = (f32[3,26,1,128]{3,1,2,0:T(8,128)}, f32[3,26,1,128]{3,1,2,0:T(8,128)}, u32[]{:S(2)}, u32[]{:S(2)}) collective-permute-start(f32[3,26,1,128]{3,1,2,0:T(8,128)} %get-tuple-element.31), channel_id=1, source_target_pairs={{0,1},{1,0},{2,3},{3,2},{4,5},{5,4},{6,7},{7,6},{8,9},{9,8},{10,11... | collective-permute-start | bytes 119816 | tf_op jit(solution)/shard_map/ppermute | solution.py:16
  152.2 25.5 %copy-start.31 = (f32[1,24,32,1]{3,1,2,0:T(8,128)S(1)}, f32[1,24,32,1]{3,1,2,0:T(8,128)}, u32[]{:S(2)}) copy-start(f32[1,24,32,1]{3,1,2,0:T(8,128)} %copy.249) | copy-start | bytes 9220
  152.2 71.6 %all-gather.11.cloned.1.call-start = ((), (), s32[]{:S(2)}) async-start(), calls=%async_computation.2 | async-start | bytes 1531904 | tf_op jit(solution)/shard_map/all_gather | solution.py:177
  154.3 23.4 %copy-start.32 = (f32[1,24,32,1]{3,1,2,0:T(8,128)S(1)}, f32[1,24,32,1]{3,1,2,0:T(8,128)}, u32[]{:S(2)}) copy-start(f32[1,24,32,1]{3,1,2,0:T(8,128)} %copy.250) | copy-start | bytes 9220
  154.3 23.4 %copy-start.35 = (f32[1,24,32,126]{3,1,2,0:T(8,128)S(1)}, f32[1,24,32,126]{3,1,2,0:T(8,128)}, u32[]{:S(2)}) copy-start(f32[1,24,32,126]{3,1,2,0:T(8,128)} %fusion.29) | copy-start | bytes 1161220
  184.4 64.0 %all-reduce.11.cloned.1.call-start = ((), (), s32[]{:S(2)}) async-start(), calls=%async_computation.5 | async-start | bytes 360448
  187.3 15.9 %collective-permute-start.8 = (f32[3,1,32,128]{3,1,2,0:T(1,128)}, f32[3,1,32,128]{3,1,2,0:T(1,128)}, u32[]{:S(2)}, u32[]{:S(2)}) collective-permute-start(f32[3,1,32,128]{3,1,2,0:T(1,128)} %get-tuple-element.34), channel_id=1, source_target_pairs={{0,2},{2,4},{4,6},{6,8},{8,10},{10,12},{12,14},{14,16},{16,18},{18... | collective-permute-start | bytes 147464 | tf_op jit(solution)/shard_map/ppermute | solution.py:16
  187.3 15.9 %collective-permute-start.9 = (f32[3,1,32,128]{3,1,2,0:T(1,128)}, f32[3,1,32,128]{3,1,2,0:T(1,128)}, u32[]{:S(2)}, u32[]{:S(2)}) collective-permute-start(f32[3,1,32,128]{3,1,2,0:T(1,128)} %get-tuple-element.35), channel_id=1, source_target_pairs={{2,0},{4,2},{6,4},{8,6},{10,8},{12,10},{14,12},{16,14},{18,16},{20... | collective-permute-start | bytes 147464 | tf_op jit(solution)/shard_map/ppermute | solution.py:17
  196.2 7.1 %copy-start.7 = (f32[1,24,32,128]{3,1,2,0:T(8,128)S(1)}, f32[1,24,32,128]{3,1,2,0:T(8,128)}, u32[]{:S(2)}) copy-start(f32[1,24,32,128]{3,1,2,0:T(8,128)} %copy-done.5) | copy-start | bytes 1179652
  204.4 21.7 %copy-start.59 = (f32[176]{0:T(256)S(1)}, f32[176]{0:T(256)}, u32[]{:S(2)}) copy-start(f32[176]{0:T(256)} %get-tuple-element.9) | copy-start | bytes 2116
  204.5 21.7 %copy-start.61 = (pred[176]{0:T(512)(128)(4,1)S(1)}, pred[176]{0:T(512)(128)(4,1)}, u32[]{:S(2)}) copy-start(pred[176]{0:T(512)(128)(4,1)} %get-tuple-element.11) | copy-start | bytes 532
  204.5 22.8 %collective-permute-start.10 = (f32[3,26,1,128]{3,1,2,0:T(8,128)S(1)}, f32[3,26,1,128]{3,1,2,0:T(8,128)S(1)}, u32[]{:S(2)}, u32[]{:S(2)}) collective-permute-start(f32[3,26,1,128]{3,1,2,0:T(8,128)S(1)} %get-tuple-element.28), channel_id=1, source_target_pairs={{1,0},{0,1},{3,2},{2,3},{5,4},{4,5},{7,6},{6,7},{9,8},{8,9},{11,10... | collective-permute-start | bytes 119816 | tf_op jit(solution)/shard_map/ppermute | solution.py:17
  204.7 23.2 %collective-permute-start.11 = (f32[3,26,1,128]{3,1,2,0:T(8,128)S(1)}, f32[3,26,1,128]{3,1,2,0:T(8,128)}, u32[]{:S(2)}, u32[]{:S(2)}) collective-permute-start(f32[3,26,1,128]{3,1,2,0:T(8,128)S(1)} %get-tuple-element.29), channel_id=1, source_target_pairs={{0,1},{1,0},{2,3},{3,2},{4,5},{5,4},{6,7},{7,6},{8,9},{9,8},{10,11... | collective-permute-start | bytes 119816 | tf_op jit(solution)/shard_map/ppermute | solution.py:16
  228.0 26.5 %copy-start.27 = (f32[24,32,1]{2,0,1:T(8,128)S(1)}, f32[24,32,1]{2,0,1:T(8,128)}, u32[]{:S(2)}) copy-start(f32[24,32,1]{2,0,1:T(8,128)} %get-tuple-element.40) | copy-start | bytes 9220
  (58 other events, 165.2 us)
Sparse Core Ops, SparseCore 0:
  13.5 41.9 all-gather.6
  77.3 21.0 all-reduce.6
  109.4 39.2 all-gather.8
  152.4 20.9 all-reduce.8
  184.5 39.2 all-gather.10
  227.4 20.9 all-reduce.10
where the time goes:
time: 268 us; the launch traced here: 266 us
  waiting for transfers between devices  88.1 us (33%)
  other arithmetic  78.7 us (29%)
  local copies, waits for them, and re-layouts  63.3 us (24%)
  starting transfers between devices  20.7 us (8%)
  between operations  15.4 us (6%)
    unnamed x9, waiting for transfers between devices  56.7 us
    all_gather x3, waiting for transfers between devices, tendency(): gathered = lax.all_gather(own_pack[None], 'pty', axis=0, tiled=True)  31.4 us
    ppermute x6, starting transfers between devices, padded(): after = lax.ppermute(initial, axis, down)  16.3 us
    unnamed x11, other arithmetic  12 us
    concatenate x6, local copies, waits for them, and re-layouts, level_diff(): return jnp.concatenate([lowest, middle, highest], axis=-1)  9.38 us
    unnamed x145, local copies, waits for them, and re-layouts  8.94 us
    gather x3, local copies, waits for them, and re-layouts, tendency(): jnp.take(flat_pack, picks, axis=0)  7.72 us
    another operation x6, other arithmetic, tendency(): horizontal = jnp.stack([vel_u, vel_v, pressure])  7.39 us
  transfers between devices with their start and end apart: 18, of which 5 were waited for; matrix products, arithmetic and copies ran while one was open for 39% of the time, Pallas kernels for 0%

commit v1 on v0

v1 whole, which is shorter than its diff:
```python
import functools

import jax
import jax.numpy as jnp
from jax import lax
from jax.experimental import pallas as pl
from jax.experimental.pallas import tpu as pltpu
from jax.sharding import PartitionSpec as P

STEP = 0.5
MESH = pl.DeviceIdType.MESH
ORDER = (0, 3, 1, 2, 4)
U, PR, V, W, B = range(5)
(SEND_UP, RECV_UP, SEND_DN, RECV_DN, SEND_L, RECV_L, SEND_R, RECV_R, ONE_C, ONE_C2, ONE_R,
 ONE_R2, TABLE, TWO, BACK_C, BACK_R, LOAD) = range(17)


def divide(x, d, limit):
    if d & (d - 1) == 0:
        return x >> (d.bit_length() - 1)
    factor = (1 << 16) // d + 1
    assert all((i * factor) >> 16 == i // d for i in range(limit)) and limit * factor < 2**31
    return (x * factor) >> 16


def kernel(n, t_count, rows, cols, levels, state, speed, freq, adj, out, buf, col, row, halo,
           tab, pick, back_c, back_r, junk, junk2, speed_v, work, sems):
    panel = cols * t_count
    total = 6 * panel
    shift = rows // 2
    row_blocks, col_blocks = rows // 4, cols // 4
    blocks = panel // 4
    groups = blocks // 2
    pairs = n // 4
    stride = max(1, t_count // -(-groups // pairs))
    edges = [(k * panel + shift) // rows for k in range(6)]
    places = [(k * panel + shift) % rows for k in range(6)]
    mask = sum(1 << m for m in range(n // 2) if 2 * m in edges)

    pty = lax.axis_index("pty")
    tx = lax.axis_index("tx")
    up = jnp.where(pty == 0, n - 1, pty - 1)
    down = jnp.where(pty == n - 1, 0, pty + 1)
    at_west = tx == 0
    at_east = tx == t_count - 1
    on_edge = at_west | at_east

    first_row = jnp.int32(-1)
    start_panel = jnp.int32(0)
    for k in range(6):
        first_row = jnp.where(pty == edges[k], places[k], first_row)
        start_panel = jnp.where(pty == edges[k], k, start_panel)
    end_panel = jnp.where(start_panel == 0, 5, start_panel - 1)
    has_start = first_row >= 0

    def holder(half, group):
        pair = group % pairs if pairs & (pairs - 1) else group & (pairs - 1)
        place = half * pairs + pair
        return (2 * place + ((mask >> place) & 1), divide(group, pairs, 4096) * stride)

    my_place = pty >> 1
    my_half = divide(my_place, pairs, 4096)
    my_pair = my_place - my_half * pairs
    my_group = divide(tx, stride, 4096) * pairs + my_pair
    is_holder = (
        ((pty & 1) == ((mask >> my_place) & 1))
        & (tx == divide(tx, stride, 4096) * stride)
        & (my_group < groups)
    )

    def push(src, dst, spare, send, recv, there):
        same = (there[0] == pty) & (there[1] == tx)

        @pl.when(same)
        def _():
            pltpu.make_async_copy(src, dst, recv).start()
            pltpu.make_async_copy(src, spare, send).start()

        @pl.when(jnp.logical_not(same))
        def _():
            pltpu.make_async_remote_copy(
                src_ref=src, dst_ref=dst, send_sem=send, recv_sem=recv,
                device_id=there, device_id_type=MESH,
            ).start()

    def done(ref, sem):
        pltpu.make_async_copy(ref, ref, sem).wait()

    loads = [
        pltpu.make_async_copy(state.at[ORDER[f]], buf.at[0, f, pl.ds(1, rows)], sems.at[LOAD, 0])
        for f in range(5)
    ]
    for copy in loads:
        copy.start()
    load_speed = pltpu.make_async_copy(speed, speed_v, sems.at[LOAD, 1])
    load_speed.start()
    done(buf.at[0, :, pl.ds(1, rows)], sems.at[LOAD, 0])

    lane = lax.broadcasted_iota(jnp.int32, (cols, levels), 1)
    line = lax.broadcasted_iota(jnp.int32, (cols, levels), 0)
    low, high = lane == 0, lane == levels - 1
    lev_half = jnp.where(low | high, 1.0, 0.5).astype(jnp.float32)
    west_line, east_line = line == 0, line == cols - 1
    col_half = jnp.where((west_line & at_west) | (east_line & at_east), 1.0, 0.5).astype(jnp.float32)
    sub = lax.broadcasted_iota(jnp.int32, (8, levels), 0)
    west_sign = jnp.where(at_west, -1.0, 1.0).astype(jnp.float32)

    def row_sends(s, there, src_row, dst_row, send, recv):
        return pltpu.make_async_remote_copy(
            src_ref=buf.at[s, pl.ds(0, 2), src_row], dst_ref=buf.at[s, pl.ds(0, 2), dst_row],
            send_sem=sems.at[send, s], recv_sem=sems.at[recv, s],
            device_id=(there, tx), device_id_type=MESH,
        )

    def col_sends(s, there, side, send, recv):
        return pltpu.make_async_remote_copy(
            src_ref=col.at[s, side], dst_ref=halo.at[s, 1 - side],
            send_sem=sems.at[send, s], recv_sem=sems.at[recv, s],
            device_id=(pty, there), device_id_type=MESH,
        )

    def stage(s, carry):
        weight_base = jnp.where(s == 0, 0.0, jnp.where(s == 1, 0.75, 1.0 / 3.0)).astype(jnp.float32)
        weight_new = jnp.where(s == 0, 1.0, jnp.where(s == 1, 0.25, 2.0 / 3.0)).astype(jnp.float32)
        weight_rate = weight_new * STEP

        def pack_col(ib, carry):
            for side in range(2):
                j = 0 if side == 0 else cols - 1
                for t in range(4):
                    i = 1 + 4 * ib + t
                    p = buf[s, PR, i, j : j + 1]
                    v = buf[s, V, i, j : j + 1]
                    col[s, side, ib, t : t + 1] = p
                    col[s, side, ib, 4 + t : 5 + t] = v * west_sign if side == 0 else v
            return carry

        lax.fori_loop(0, row_blocks, pack_col, 0)

        @pl.when(has_start)
        def _():
            for e in range(2):
                i = first_row + 1 - e
                for m in range(col_blocks // 2):
                    p = buf[s, PR, i, 8 * m : 8 * m + 8]
                    u = buf[s, U, i, 8 * m : 8 * m + 8]
                    if e == 0:
                        u = -u
                    row[s, e * col_blocks + 2 * m] = jnp.where(sub < 4, p, pltpu.roll(u, 4, 0))
                    row[s, e * col_blocks + 2 * m + 1] = jnp.where(sub < 4, pltpu.roll(p, 4, 0), u)

        @pl.when(on_edge)
        def _():
            side = jnp.where(at_west, 0, 1)
            edge = jnp.where(at_west, 3, 1)

            def one(ib, carry):
                place = pty * rows + 4 * ib - shift
                place = jnp.where(place < 0, place + total, place)
                k = divide(place, panel, total)
                b = (place - k * panel) >> 2
                far = b >= groups
                slot = (k * 4 + edge) * 2 + jnp.where(far, 1, 0)
                group = jnp.where(far, blocks - 1 - b, b)
                for half in range(2):
                    push(col.at[s, side, ib], tab.at[s, slot], junk.at[s, half, ib],
                         sems.at[ONE_C + half, s], sems.at[TABLE, s], holder(half, group))
                return carry

            lax.fori_loop(0, row_blocks, one, 0)

        @pl.when(has_start)
        def _():
            def one(m, carry):
                b = tx * col_blocks + m
                far = b >= groups
                group = jnp.where(far, blocks - 1 - b, b)
                for e in range(2):
                    k = start_panel if e == 0 else end_panel
                    slot = (k * 4 + 2 * e) * 2 + jnp.where(far, 1, 0)
                    for half in range(2):
                        push(row.at[s, e * col_blocks + m], tab.at[s, slot],
                             junk.at[s, half, row_blocks + e * col_blocks + m],
                             sems.at[ONE_R + half, s], sems.at[TABLE, s], holder(half, group))
                return carry

            lax.fori_loop(0, col_blocks, one, 0)

        row_sends(s, up, 1, rows + 1, SEND_UP, RECV_UP).start()
        row_sends(s, down, rows, 0, SEND_DN, RECV_DN).start()

        @pl.when(tx > 0)
        def _():
            col_sends(s, tx - 1, 0, SEND_L, RECV_L).start()

        @pl.when(tx < t_count - 1)
        def _():
            col_sends(s, tx + 1, 1, SEND_R, RECV_R).start()

        def vertical(ib, carry):
            rate = weight_rate * freq[0:1]
            for t in range(4):
                i = 1 + 4 * ib + t
                p, w, b = buf[s, PR, i], buf[s, W, i], buf[s, B, i]
                above = jnp.where(high, p, pltpu.roll(p, levels - 1, 1))
                below = jnp.where(low, p, pltpu.roll(p, 1, 1))
                diff = lev_half * (above - below)
                buf[s + 1, W, i] = weight_base * buf[0, W, i] + (weight_new * w + weight_rate * (b - diff))
                buf[s + 1, B, i] = weight_base * buf[0, B, i] + (weight_new * b - rate * w)
            return carry

        lax.fori_loop(0, row_blocks, vertical, 0)

        @pl.when(is_holder)
        def _():
            done(tab.at[s], sems.at[TABLE, s])
            work[...] = tab[s]

            def one(kk, carry):
                k = my_half * 3 + kk
                for e in range(4):
                    entry = (k * 4 + e) * 3
                    partner = (adj[entry] * 4 + adj[entry + 1]) * 2
                    flip = adj[entry + 2]
                    for far in range(2):
                        b = my_group if far == 0 else blocks - 1 - my_group
                        value = work[partner + (flip if far == 0 else 1 - flip)]
                        two = jnp.where((sub & 2) == 0, pltpu.roll(value, 6, 0), pltpu.roll(value, 2, 0))
                        turned = jnp.where((sub & 1) == 0, pltpu.roll(two, 7, 0), pltpu.roll(two, 1, 0))
                        slot = kk * 8 + e * 2 + far
                        pick[s, slot] = jnp.where(flip == 1, turned, value)
                        if e == 1 or e == 3:
                            place = k * panel + 4 * b + shift
                            place = jnp.where(place >= total, place - total, place)
                            owner = divide(place, rows, total)
                            index = (place - owner * rows) >> 2
                            push(pick.at[s, slot], back_c.at[s, index], junk2.at[s, slot],
                                 sems.at[TWO, s], sems.at[BACK_C, s],
                                 (owner, t_count - 1 if e == 1 else 0))
                        else:
                            place = k * panel + shift + (0 if e == 0 else panel - 1)
                            place = jnp.where(place >= total, place - total, place)
                            owner = divide(place, rows, total)
                            owner_tx = divide(b, col_blocks, total)
                            index = (e // 2) * col_blocks + b - owner_tx * col_blocks
                            push(pick.at[s, slot], back_r.at[s, index], junk2.at[s, slot],
                                 sems.at[TWO, s], sems.at[BACK_R, s], (owner, owner_tx))
                return carry

            lax.fori_loop(0, 3, one, 0)

        row_sends(s, up, 1, rows + 1, SEND_UP, RECV_UP).wait_recv()
        row_sends(s, down, rows, 0, SEND_DN, RECV_DN).wait_recv()

        @pl.when(tx > 0)
        def _():
            done(halo.at[s, 0], sems.at[RECV_R, s])

        @pl.when(tx < t_count - 1)
        def _():
            done(halo.at[s, 1], sems.at[RECV_L, s])

        @pl.when(s == 0)
        def _():
            load_speed.wait()

        def horizontal(ib, carry):
            for t in range(4):
                i = 1 + 4 * ib + t
                is_start, is_end = i - 1 == first_row, i == first_row
                row_half = jnp.where(is_start | is_end, 1.0, 0.5).astype(jnp.float32)
                u, p, v, w = buf[s, U, i], buf[s, PR, i], buf[s, V, i], buf[s, W, i]

                def along_rows(f, here):
                    after = jnp.where(is_end, here, buf[s, f, i + 1])
                    before = jnp.where(is_start, here, buf[s, f, i - 1])
                    return row_half * (after - before)

                def along_cols(here, offset):
                    left = halo[s, 0, ib, offset + t : offset + t + 1]
                    right = halo[s, 1, ib, offset + t : offset + t + 1]
                    left = jnp.where(at_west, here[0:1], left)
                    right = jnp.where(at_east, here[cols - 1 :], right)
                    after = jnp.where(east_line, right, pltpu.roll(here, cols - 1, 0))
                    before = jnp.where(west_line, left, pltpu.roll(here, 1, 0))
                    return col_half * (after - before)

                above = jnp.where(high, -w, pltpu.roll(w, levels - 1, 1))
                below = jnp.where(low, -w, pltpu.roll(w, 1, 1))
                wall = lev_half * (above - below)
                buf[s + 1, U, i] = weight_base * buf[0, U, i] + (
                    weight_new * u - weight_rate * along_rows(PR, p))
                buf[s + 1, V, i] = weight_base * buf[0, V, i] + (
                    weight_new * v - weight_rate * along_cols(p, 0))
                buf[s + 1, PR, i] = weight_base * buf[0, PR, i] + (
                    weight_new * p - (weight_rate * speed_v[i - 1]) * (
                        along_rows(U, u) + along_cols(v, 4) + wall))
            return carry

        lax.fori_loop(0, row_blocks, horizontal, 0)

        @pl.when(has_start)
        def _():
            done(back_r.at[s], sems.at[BACK_R, s])
            for e in range(2):
                i = first_row + 1 - e
                sign = -1.0 if e == 0 else 1.0
                for m in range(col_blocks // 2):
                    one, two = back_r[s, e * col_blocks + 2 * m], back_r[s, e * col_blocks + 2 * m + 1]
                    p_there = jnp.where(sub < 4, one, pltpu.roll(two, 4, 0))
                    n_there = jnp.where(sub < 4, pltpu.roll(one, 4, 0), two)
                    at = pl.ds(8 * m, 8)
                    n_here = sign * buf[s, U, i, at]
                    buf[s + 1, PR, i, at] += weight_rate * speed_v[i - 1, at] * (n_here + n_there)
                    buf[s + 1, U, i, at] += (sign * weight_rate) * (buf[s, PR, i, at] - p_there)

        for side in range(2):
            @pl.when(at_west if side == 0 else at_east)
            def _():
                done(back_c.at[s], sems.at[BACK_C, s])
                sign = -1.0 if side == 0 else 1.0
                j = 0 if side == 0 else cols - 1

                def one(ib, carry):
                    for t in range(4):
                        i = 1 + 4 * ib + t
                        p_here = col[s, side, ib, t : t + 1]
                        n_here = col[s, side, ib, 4 + t : 5 + t]
                        p_there = back_c[s, ib, t : t + 1]
                        n_there = back_c[s, ib, 4 + t : 5 + t]
                        buf[s + 1, PR, i, j : j + 1] += (
                            weight_rate * speed_v[i - 1, j : j + 1] * (n_here + n_there))
                        buf[s + 1, V, i, j : j + 1] += (sign * weight_rate) * (p_here - p_there)
                    return carry

                lax.fori_loop(0, row_blocks, one, 0)

        return carry

    @pl.when(at_west)
    def _():
        halo[:, 0] = jnp.zeros((3, row_blocks, 8, levels), jnp.float32)

    @pl.when(at_east)
    def _():
        halo[:, 1] = jnp.zeros((3, row_blocks, 8, levels), jnp.float32)

    lax.fori_loop(0, 3, stage, 0)

    stores = [
        pltpu.make_async_copy(buf.at[3, f, pl.ds(1, rows)], out.at[ORDER[f]], sems.at[LOAD, 2])
        for f in range(5)
    ]
    for copy in stores:
        copy.start()

    def finish(s, carry):
        row_sends(s, up, 1, rows + 1, SEND_UP, RECV_UP).wait_send()
        row_sends(s, down, rows, 0, SEND_DN, RECV_DN).wait_send()

        @pl.when(tx > 0)
        def _():
            done(col.at[s, 0], sems.at[SEND_L, s])

        @pl.when(tx < t_count - 1)
        def _():
            done(col.at[s, 1], sems.at[SEND_R, s])

        for half in range(2):
            @pl.when(on_edge)
            def _():
                done(col.at[s, 0], sems.at[ONE_C + half, s])

            @pl.when(has_start)
            def _():
                done(row.at[s], sems.at[ONE_R + half, s])

        @pl.when(is_holder)
        def _():
            done(pick.at[s], sems.at[TWO, s])

        return carry

    lax.fori_loop(0, 3, finish, 0)
    done(buf.at[3, :, pl.ds(1, rows)], sems.at[LOAD, 2])


def on_device(n, t_count, state, speed, freq, adjacency):
    _, rows, cols, levels = state.shape
    rb, cb = rows // 4, cols // 4
    f32 = jnp.float32
    return pl.pallas_call(
        functools.partial(kernel, n, t_count, rows, cols, levels),
        out_shape=jax.ShapeDtypeStruct(state.shape, f32),
        in_specs=[
            pl.BlockSpec(memory_space=pl.ANY),
            pl.BlockSpec(memory_space=pl.ANY),
            pl.BlockSpec(memory_space=pltpu.VMEM),
            pl.BlockSpec(memory_space=pltpu.SMEM),
        ],
        out_specs=pl.BlockSpec(memory_space=pl.ANY),
        scratch_shapes=[
            pltpu.VMEM((4, 5, rows + 2, cols, levels), f32),
            pltpu.VMEM((3, 2, rb, 8, levels), f32),
            pltpu.VMEM((3, 2 * cb, 8, levels), f32),
            pltpu.VMEM((3, 2, rb, 8, levels), f32),
            pltpu.VMEM((3, 48, 8, levels), f32),
            pltpu.VMEM((3, 24, 8, levels), f32),
            pltpu.VMEM((3, rb, 8, levels), f32),
            pltpu.VMEM((3, 2 * cb, 8, levels), f32),
            pltpu.VMEM((3, 2, rb + 2 * cb, 8, levels), f32),
            pltpu.VMEM((3, 24, 8, levels), f32),
            pltpu.VMEM((rows, cols, levels), f32),
            pltpu.VMEM((48, 8, levels), f32),
            pltpu.SemaphoreType.DMA((17, 3)),
        ],
        compiler_params=pltpu.CompilerParams(
            has_side_effects=True, vmem_limit_bytes=32 * 1024 * 1024
        ),
    )(state, speed, freq.reshape(1, levels), adjacency.reshape(-1))


def solution(mesh):
    in_specs = (P(None, "pty", "tx", None), P("pty", "tx", None), P(), P())
    out_specs = P(None, "pty", "tx", None)
    return jax.shard_map(
        functools.partial(on_device, mesh.shape["pty"], mesh.shape["tx"]),
        mesh=mesh, in_specs=in_specs, out_specs=out_specs, check_vma=False,
    )
```

time: 268 us -> 49.8 us (0.19)
  waiting for transfers between devices: 88.1 us -> 0 us
  other arithmetic: 78.7 us -> 0 us
  local copies, waits for them, and re-layouts: 63.3 us -> 5.36 us
  Pallas kernels: 0 us -> 44.2 us
  starting transfers between devices: 20.7 us -> 0 us
  between operations: 15.4 us -> 0.02 us
    unnamed x9 -> x0, waiting for transfers between devices: 56.7 us -> none
    pallas_call x0 -> x1, Pallas kernels: none -> 44.2 us  [on_device(): pl.pallas_call(functools.partial(kernel, n, t_count, rows, cols, levels),...]
    all_gather x3 -> x0, waiting for transfers between devices: 31.4 us -> none  [tendency(): gathered = lax.all_gather(own_pack[None], 'pty', axis=0, tiled=True)]
    ppermute x12 -> x0, starting transfers between devices: 20.5 us -> none  [the longest x6 16.3 us: padded(): after = lax.ppermute(initial, axis, down)]
    concatenate x16 -> x0, local copies, waits for them, and re-layouts: 14.5 us -> none  [the longest x6 9.38 us: level_diff(): return jnp.concatenate([lowest, middle, highest], axis=-1)]
    unnamed x11 -> x0, other arithmetic: 12 us -> none
    select_n x9 -> x0, other arithmetic: 11.4 us -> none  [the longest x3 6.03 us: tendency(): jnp.where(col_start, col_after - col_here, jnp.where(col_end, col_here -...]
    another operation x18 -> x0, other arithmetic: 11 us -> none  [the longest x6 7.39 us: tendency(): horizontal = jnp.stack([vel_u, vel_v, pressure])]
  transfers between devices with their start and end apart: 18 -> 0, of which waited for: 5 -> 0; matrix products, arithmetic and copies ran while one was open for 39% -> 0% of each run, Pallas kernels for 0% -> 0%
where the time goes in v1:
time: 49.8 us; the launch traced here: 49.6 us
  Pallas kernels  44.2 us (89%)
  local copies, waits for them, and re-layouts  5.36 us (11%)
    pallas_call x1, Pallas kernels, on_device(): pl.pallas_call(functools.partial(kernel, n, t_count, rows, cols, levels),...  44.2 us
    unnamed x8, local copies, waits for them, and re-layouts  5.26 us

profile of v1, /device:TPU:0, one launch (start us, length us, event | category | flops | bytes accessed | tf_op | source)
XLA Modules:
  0.0 49.6 jit_solution(10965347088699331630)
XLA Ops:
  0.0 0.8 %copy.6 = s32[6,4,3]{2,1,0:T(4,128)S(1)} copy(s32[6,4,3]{0,1,2:T(4,128)} %param.7) | data formatting | bytes 576 | tf_op args[3]
  0.8 0.1 reshape.7.adj
  0.9 0.0 copy-start
  0.9 1.5 %copy-done = f32[5,24,32,128]{3,2,1,0:T(8,128)S(1)} copy-done((f32[5,24,32,128]{3,2,1,0:T(8,128)S(1)}, f32[5,24,32,128]{3,2,1,0:T(8,128)}, u32[]{:S(2)}) %copy-start) | copy-done | bytes 1966104
  2.4 0.0 copy-start.1
  2.5 1.0 %copy-done.1 = f32[24,32,128]{2,1,0:T(8,128)S(1)} copy-done((f32[24,32,128]{2,1,0:T(8,128)S(1)}, f32[24,32,128]{2,1,0:T(8,128)}, u32[]{:S(2)}) %copy-start.1) | copy-done | bytes 393240
  3.4 0.0 copy-start.2
  3.4 0.7 %copy-done.2 = f32[128]{0:T(128)S(1)} copy-done((f32[128]{0:T(128)S(1)}, f32[128]{0:T(128)}, u32[]{:S(2)}) %copy-start.2) | copy-done | bytes 536
  4.1 44.2 %shard_map.46 = f32[5,24,32,128]{3,2,1,0:T(8,128)S(1)} custom-call(f32[5,24,32,128]{3,2,1,0:T(8,128)S(1)} %copy-done, f32[24,32,128]{2,1,0:T(8,128)S(1)} %copy-done.1, f32[1,128]{1,0:T(1,128)S(1)} %bitcast.1, s32[72]{0:T(128)S(1)} %reshape.7.adj), custom_call_target="tpu_custom_call" | custom-call | tf_op jit(solution)/shard_map/pallas_call | solution.py:392
  48.3 1.3 %copy.8 = f32[5,24,32,128]{3,2,1,0:T(8,128)} copy(f32[5,24,32,128]{3,2,1,0:T(8,128)S(1)} %shard_map.46) | data formatting | bytes 3932160
Async XLA Ops:
  0.9 1.6 %copy-start = (f32[5,24,32,128]{3,2,1,0:T(8,128)S(1)}, f32[5,24,32,128]{3,2,1,0:T(8,128)}, u32[]{:S(2)}) copy-start(f32[5,24,32,128]{3,2,1,0:T(8,128)} %state.1) | copy-start | bytes 5898244
  2.4 1.0 %copy-start.1 = (f32[24,32,128]{2,1,0:T(8,128)S(1)}, f32[24,32,128]{2,1,0:T(8,128)}, u32[]{:S(2)}) copy-start(f32[24,32,128]{2,1,0:T(8,128)} %speed.1) | copy-start | bytes 1179652
  3.4 0.7 %copy-start.2 = (f32[128]{0:T(128)S(1)}, f32[128]{0:T(128)}, u32[]{:S(2)}) copy-start(f32[128]{0:T(128)} %param.6) | copy-start | bytes 1540

commit v2 on v1

--- a/solution.py
+++ b/solution.py
@@ -24,7 +24,7 @@
 
 
 def kernel(n, t_count, rows, cols, levels, state, speed, freq, adj, out, buf, col, row, halo,
-           tab, pick, back_c, back_r, junk, junk2, speed_v, work, sems):
+           tab, pick, back_c, back_r, junk, junk_r, junk2, speed_v, freq_v, work, sems):
     panel = cols * t_count
     total = 6 * panel
     shift = rows // 2
@@ -50,7 +50,6 @@
     for k in range(6):
         first_row = jnp.where(pty == edges[k], places[k], first_row)
         start_panel = jnp.where(pty == edges[k], k, start_panel)
-    end_panel = jnp.where(start_panel == 0, 5, start_panel - 1)
     has_start = first_row >= 0
 
     def holder(half, group):
@@ -86,6 +85,17 @@
     def done(ref, sem):
         pltpu.make_async_copy(ref, ref, sem).wait()
 
+    barrier = pltpu.get_barrier_semaphore()
+    for a in range(n):
+        for c in range(t_count):
+            if a == 0 and c == 0:
+                continue
+            there = pty + a
+            there = jnp.where(there >= n, there - n, there)
+            there_tx = tx + c
+            there_tx = jnp.where(there_tx >= t_count, there_tx - t_count, there_tx)
+            pl.semaphore_signal(barrier, inc=1, device_id=(there, there_tx), device_id_type=MESH)
+
     loads = [
         pltpu.make_async_copy(state.at[ORDER[f]], buf.at[0, f, pl.ds(1, rows)], sems.at[LOAD, 0])
         for f in range(5)
@@ -94,6 +104,8 @@
         copy.start()
     load_speed = pltpu.make_async_copy(speed, speed_v, sems.at[LOAD, 1])
     load_speed.start()
+    load_freq = pltpu.make_async_copy(freq, freq_v, sems.at[LOAD, 2])
+    load_freq.start()
     done(buf.at[0, :, pl.ds(1, rows)], sems.at[LOAD, 0])
 
     lane = lax.broadcasted_iota(jnp.int32, (cols, levels), 1)
@@ -146,13 +158,17 @@
                     u = buf[s, U, i, 8 * m : 8 * m + 8]
                     if e == 0:
                         u = -u
-                    row[s, e * col_blocks + 2 * m] = jnp.where(sub < 4, p, pltpu.roll(u, 4, 0))
-                    row[s, e * col_blocks + 2 * m + 1] = jnp.where(sub < 4, pltpu.roll(p, 4, 0), u)
+                    row[s, e, 2 * m] = jnp.where(sub < 4, p, pltpu.roll(u, 4, 0))
+                    row[s, e, 2 * m + 1] = jnp.where(sub < 4, pltpu.roll(p, 4, 0), u)
+
+        @pl.when(s == 0)
+        def _():
+            pl.semaphore_wait(barrier, n * t_count - 1)
+            load_freq.wait()
 
         @pl.when(on_edge)
         def _():
             side = jnp.where(at_west, 0, 1)
-            edge = jnp.where(at_west, 3, 1)
 
             def one(ib, carry):
                 place = pty * rows + 4 * ib - shift
@@ -160,7 +176,7 @@
                 k = divide(place, panel, total)
                 b = (place - k * panel) >> 2
                 far = b >= groups
-                slot = (k * 4 + edge) * 2 + jnp.where(far, 1, 0)
+                slot = 24 + k * 4 + jnp.where(at_west, 2, 0) + jnp.where(far, 1, 0)
                 group = jnp.where(far, blocks - 1 - b, b)
                 for half in range(2):
                     push(col.at[s, side, ib], tab.at[s, slot], junk.at[s, half, ib],
@@ -175,13 +191,10 @@
                 b = tx * col_blocks + m
                 far = b >= groups
                 group = jnp.where(far, blocks - 1 - b, b)
-                for e in range(2):
-                    k = start_panel if e == 0 else end_panel
-                    slot = (k * 4 + 2 * e) * 2 + jnp.where(far, 1, 0)
-                    for half in range(2):
-                        push(row.at[s, e * col_blocks + m], tab.at[s, slot],
-                             junk.at[s, half, row_blocks + e * col_blocks + m],
-                             sems.at[ONE_R + half, s], sems.at[TABLE, s], holder(half, group))
+                slot = (start_panel * 2 + jnp.where(far, 1, 0)) * 2
+                for half in range(2):
+                    push(row.at[s, :, m], tab.at[s, pl.ds(slot, 2)], junk_r.at[s, half, m],
+                         sems.at[ONE_R + half, s], sems.at[TABLE, s], holder(half, group))
                 return carry
 
             lax.fori_loop(0, col_blocks, one, 0)
@@ -198,7 +211,7 @@
             col_sends(s, tx + 1, 1, SEND_R, RECV_R).start()
 
         def vertical(ib, carry):
-            rate = weight_rate * freq[0:1]
+            rate = weight_rate * freq_v[0:1]
             for t in range(4):
                 i = 1 + 4 * ib + t
                 p, w, b = buf[s, PR, i], buf[s, W, i], buf[s, B, i]
@@ -218,33 +231,41 @@
 
             def one(kk, carry):
                 k = my_half * 3 + kk
-                for e in range(4):
-                    entry = (k * 4 + e) * 3
-                    partner = (adj[entry] * 4 + adj[entry + 1]) * 2
-                    flip = adj[entry + 2]
-                    for far in range(2):
-                        b = my_group if far == 0 else blocks - 1 - my_group
-                        value = work[partner + (flip if far == 0 else 1 - flip)]
-                        two = jnp.where((sub & 2) == 0, pltpu.roll(value, 6, 0), pltpu.roll(value, 2, 0))
-                        turned = jnp.where((sub & 1) == 0, pltpu.roll(two, 7, 0), pltpu.roll(two, 1, 0))
-                        slot = kk * 8 + e * 2 + far
-                        pick[s, slot] = jnp.where(flip == 1, turned, value)
-                        if e == 1 or e == 3:
-                            place = k * panel + 4 * b + shift
-                            place = jnp.where(place >= total, place - total, place)
-                            owner = divide(place, rows, total)
-                            index = (place - owner * rows) >> 2
-                            push(pick.at[s, slot], back_c.at[s, index], junk2.at[s, slot],
-                                 sems.at[TWO, s], sems.at[BACK_C, s],
-                                 (owner, t_count - 1 if e == 1 else 0))
-                        else:
-                            place = k * panel + shift + (0 if e == 0 else panel - 1)
-                            place = jnp.where(place >= total, place - total, place)
-                            owner = divide(place, rows, total)
-                            owner_tx = divide(b, col_blocks, total)
-                            index = (e // 2) * col_blocks + b - owner_tx * col_blocks
-                            push(pick.at[s, slot], back_r.at[s, index], junk2.at[s, slot],
-                                 sems.at[TWO, s], sems.at[BACK_R, s], (owner, owner_tx))
+                before = jnp.where(k == 0, 5, k - 1)
+
+                def choose(panel_here, edge, far):
+                    entry = (panel_here * 4 + edge) * 3
+                    other, face, flip = adj[entry], adj[entry + 1], adj[entry + 2]
+                    side = flip if far == 0 else 1 - flip
+                    bound = jnp.where(face == 2, jnp.where(other == 5, 0, other + 1), other)
+                    index = jnp.where((face & 1) == 0, bound * 4 + side * 2 + (face >> 1),
+                                      24 + other * 4 + (face >> 1) * 2 + side)
+                    value = work[index]
+                    two = jnp.where((sub & 2) == 0, pltpu.roll(value, 6, 0), pltpu.roll(value, 2, 0))
+                    turned = jnp.where((sub & 1) == 0, pltpu.roll(two, 7, 0), pltpu.roll(two, 1, 0))
+                    return jnp.where(flip == 1, turned, value)
+
+                for far in range(2):
+                    b = my_group if far == 0 else blocks - 1 - my_group
+                    place = k * panel + shift
+                    owner = divide(place, rows, total)
+                    owner_tx = divide(b, col_blocks, total)
+                    slot = (kk * 2 + far) * 2
+                    pick[s, slot] = choose(k, 0, far)
+                    pick[s, slot + 1] = choose(before, 2, far)
+                    push(pick.at[s, pl.ds(slot, 2)], back_r.at[s, :, b - owner_tx * col_blocks],
+                         junk2.at[s, pl.ds(slot, 2)], sems.at[TWO, s], sems.at[BACK_R, s],
+                         (owner, owner_tx))
+                    place = k * panel + 4 * b + shift
+                    place = jnp.where(place >= total, place - total, place)
+                    owner = divide(place, rows, total)
+                    index = (place - owner * rows) >> 2
+                    for e in (1, 3):
+                        slot = 12 + kk * 4 + far * 2 + e // 2
+                        pick[s, slot] = choose(k, e, far)
+                        push(pick.at[s, slot], back_c.at[s, index], junk2.at[s, slot],
+                             sems.at[TWO, s], sems.at[BACK_C, s],
+                             (owner, t_count - 1 if e == 1 else 0))
                 return carry
 
             lax.fori_loop(0, 3, one, 0)
@@ -306,7 +327,7 @@
                 i = first_row + 1 - e
                 sign = -1.0 if e == 0 else 1.0
                 for m in range(col_blocks // 2):
-                    one, two = back_r[s, e * col_blocks + 2 * m], back_r[s, e * col_blocks + 2 * m + 1]
+                    one, two = back_r[s, e, 2 * m], back_r[s, e, 2 * m + 1]
                     p_there = jnp.where(sub < 4, one, pltpu.roll(two, 4, 0))
                     n_there = jnp.where(sub < 4, pltpu.roll(one, 4, 0), two)
                     at = pl.ds(8 * m, 8)
@@ -393,29 +414,31 @@
         functools.partial(kernel, n, t_count, rows, cols, levels),
         out_shape=jax.ShapeDtypeStruct(state.shape, f32),
         in_specs=[
-            pl.BlockSpec(memory_space=pl.ANY),
-            pl.BlockSpec(memory_space=pl.ANY),
-            pl.BlockSpec(memory_space=pltpu.VMEM),
+            pl.BlockSpec(memory_space=pltpu.HBM),
+            pl.BlockSpec(memory_space=pltpu.HBM),
+            pl.BlockSpec(memory_space=pltpu.HBM),
             pl.BlockSpec(memory_space=pltpu.SMEM),
         ],
         out_specs=pl.BlockSpec(memory_space=pl.ANY),
         scratch_shapes=[
             pltpu.VMEM((4, 5, rows + 2, cols, levels), f32),
             pltpu.VMEM((3, 2, rb, 8, levels), f32),
-            pltpu.VMEM((3, 2 * cb, 8, levels), f32),
+            pltpu.VMEM((3, 2, cb, 8, levels), f32),
             pltpu.VMEM((3, 2, rb, 8, levels), f32),
             pltpu.VMEM((3, 48, 8, levels), f32),
             pltpu.VMEM((3, 24, 8, levels), f32),
             pltpu.VMEM((3, rb, 8, levels), f32),
-            pltpu.VMEM((3, 2 * cb, 8, levels), f32),
-            pltpu.VMEM((3, 2, rb + 2 * cb, 8, levels), f32),
+            pltpu.VMEM((3, 2, cb, 8, levels), f32),
+            pltpu.VMEM((3, 2, rb, 8, levels), f32),
+            pltpu.VMEM((3, 2, cb, 2, 8, levels), f32),
             pltpu.VMEM((3, 24, 8, levels), f32),
             pltpu.VMEM((rows, cols, levels), f32),
+            pltpu.VMEM((1, levels), f32),
             pltpu.VMEM((48, 8, levels), f32),
             pltpu.SemaphoreType.DMA((17, 3)),
         ],
         compiler_params=pltpu.CompilerParams(
-            has_side_effects=True, vmem_limit_bytes=32 * 1024 * 1024
+            has_side_effects=True, collective_id=0, vmem_limit_bytes=62 * 1024 * 1024
         ),
     )(state, speed, freq.reshape(1, levels), adjacency.reshape(-1))
 

time: 49.8 us -> 42.9 us (0.86)
  Pallas kernels: 44.2 us -> 38.2 us
  local copies, waits for them, and re-layouts: 5.36 us -> 4.48 us
    pallas_call x1, Pallas kernels: 44.2 us -> 38.2 us  [on_device(): pl.pallas_call(functools.partial(kernel, n, t_count, rows, cols, levels),...]
    unnamed x8 -> x2, local copies, waits for them, and re-layouts: 5.26 us -> 3.87 us
    reshape x1, local copies, waits for them, and re-layouts: 0.1 us -> 0.62 us  [on_device(): adjacency.reshape(-1)]
where the time goes in v2:
time: 42.9 us; the launch traced here: 42.7 us
  Pallas kernels  38.2 us (89%)
  local copies, waits for them, and re-layouts  4.48 us (10%)
    pallas_call x1, Pallas kernels, on_device(): pl.pallas_call(functools.partial(kernel, n, t_count, rows, cols, levels),...  38.2 us
    unnamed x2, local copies, waits for them, and re-layouts  3.87 us

profile of v2, /device:TPU:0, one launch (start us, length us, event | category | flops | bytes accessed | tf_op | source)
XLA Modules:
  0.0 42.7 jit_solution(10404625697228321420)
XLA Ops:
  0.0 0.8 %copy.6 = s32[6,4,3]{2,1,0:T(4,128)S(1)} copy(s32[6,4,3]{0,1,2:T(4,128)} %param.7) | data formatting | bytes 576 | tf_op args[3]
  0.8 0.6 %reshape.7.adj = s32[72]{0:T(128)} reshape(s32[6,4,3]{2,1,0:T(4,128)S(1)} %copy.6) | data formatting | bytes 576 | tf_op jit(solution)/shard_map/reshape | solution.py:443
  1.4 38.2 %shard_map.46 = f32[5,24,32,128]{3,2,1,0:T(8,128)} custom-call(f32[5,24,32,128]{3,2,1,0:T(8,128)} %state.1, f32[24,32,128]{2,1,0:T(8,128)} %speed.1, f32[1,128]{1,0:T(1,128)} %bitcast.1, s32[72]{0:T(128)} %reshape.7.adj), custom_call_target="tpu_custom_call" | custom-call | tf_op jit(solution)/shard_map/pallas_call | solution.py:413
  39.6 3.1 %copy.8 = f32[5,24,32,128]{3,2,1,0:T(8,128)} copy(f32[5,24,32,128]{3,2,1,0:T(8,128)} %shard_map.46) | data formatting | bytes 3932160

commit v3 on v2

--- a/solution.py
+++ b/solution.py
@@ -52,18 +52,21 @@
         start_panel = jnp.where(pty == edges[k], k, start_panel)
     has_start = first_row >= 0
 
-    def holder(half, group):
+    first_pair = n // 8
+
+    def holder(group):
         pair = group % pairs if pairs & (pairs - 1) else group & (pairs - 1)
-        place = half * pairs + pair
+        place = first_pair + pair
         return (2 * place + ((mask >> place) & 1), divide(group, pairs, 4096) * stride)
 
     my_place = pty >> 1
-    my_half = divide(my_place, pairs, 4096)
-    my_pair = my_place - my_half * pairs
+    my_pair = my_place - first_pair
     my_group = divide(tx, stride, 4096) * pairs + my_pair
     is_holder = (
         ((pty & 1) == ((mask >> my_place) & 1))
         & (tx == divide(tx, stride, 4096) * stride)
+        & (my_pair >= 0)
+        & (my_pair < pairs)
         & (my_group < groups)
     )
 
@@ -131,6 +134,10 @@
             device_id=(pty, there), device_id_type=MESH,
         )
 
+    def store(f):
+        return pltpu.make_async_copy(
+            buf.at[3, f, pl.ds(1, rows)], out.at[ORDER[f]], sems.at[LOAD, 2 if f < W else 0])
+
     def stage(s, carry):
         weight_base = jnp.where(s == 0, 0.0, jnp.where(s == 1, 0.75, 1.0 / 3.0)).astype(jnp.float32)
         weight_new = jnp.where(s == 0, 1.0, jnp.where(s == 1, 0.25, 2.0 / 3.0)).astype(jnp.float32)
@@ -166,6 +173,20 @@
             pl.semaphore_wait(barrier, n * t_count - 1)
             load_freq.wait()
 
+        @pl.when(has_start)
+        def _():
+            def one(m, carry):
+                b = tx * col_blocks + m
+                far = b >= groups
+                group = jnp.where(far, blocks - 1 - b, b)
+                slot = (start_panel * 2 + jnp.where(far, 1, 0)) * 2
+                for half in range(1):
+                    push(row.at[s, :, m], tab.at[s, pl.ds(slot, 2)], junk_r.at[s, half, m],
+                         sems.at[ONE_R + half, s], sems.at[TABLE, s], holder(group))
+                return carry
+
+            lax.fori_loop(0, col_blocks, one, 0)
+
         @pl.when(on_edge)
         def _():
             side = jnp.where(at_west, 0, 1)
@@ -178,26 +199,12 @@
                 far = b >= groups
                 slot = 24 + k * 4 + jnp.where(at_west, 2, 0) + jnp.where(far, 1, 0)
                 group = jnp.where(far, blocks - 1 - b, b)
-                for half in range(2):
+                for half in range(1):
                     push(col.at[s, side, ib], tab.at[s, slot], junk.at[s, half, ib],
-                         sems.at[ONE_C + half, s], sems.at[TABLE, s], holder(half, group))
+                         sems.at[ONE_C + half, s], sems.at[TABLE, s], holder(group))
                 return carry
 
             lax.fori_loop(0, row_blocks, one, 0)
-
-        @pl.when(has_start)
-        def _():
-            def one(m, carry):
-                b = tx * col_blocks + m
-                far = b >= groups
-                group = jnp.where(far, blocks - 1 - b, b)
-                slot = (start_panel * 2 + jnp.where(far, 1, 0)) * 2
-                for half in range(2):
-                    push(row.at[s, :, m], tab.at[s, pl.ds(slot, 2)], junk_r.at[s, half, m],
-                         sems.at[ONE_R + half, s], sems.at[TABLE, s], holder(half, group))
-                return carry
-
-            lax.fori_loop(0, col_blocks, one, 0)
 
         row_sends(s, up, 1, rows + 1, SEND_UP, RECV_UP).start()
         row_sends(s, down, rows, 0, SEND_DN, RECV_DN).start()
@@ -224,13 +231,18 @@
 
         lax.fori_loop(0, row_blocks, vertical, 0)
 
+        @pl.when(s == 2)
+        def _():
+            for f in (W, B):
+                store(f).start()
+
         @pl.when(is_holder)
         def _():
             done(tab.at[s], sems.at[TABLE, s])
             work[...] = tab[s]
 
             def one(kk, carry):
-                k = my_half * 3 + kk
+                k = kk
                 before = jnp.where(k == 0, 5, k - 1)
 
                 def choose(panel_here, edge, far):
@@ -261,14 +273,14 @@
                     owner = divide(place, rows, total)
                     index = (place - owner * rows) >> 2
                     for e in (1, 3):
-                        slot = 12 + kk * 4 + far * 2 + e // 2
+                        slot = 24 + kk * 4 + far * 2 + e // 2
                         pick[s, slot] = choose(k, e, far)
                         push(pick.at[s, slot], back_c.at[s, index], junk2.at[s, slot],
                              sems.at[TWO, s], sems.at[BACK_C, s],
                              (owner, t_count - 1 if e == 1 else 0))
                 return carry
 
-            lax.fori_loop(0, 3, one, 0)
+            lax.fori_loop(0, 6, one, 0)
 
         row_sends(s, up, 1, rows + 1, SEND_UP, RECV_UP).wait_recv()
         row_sends(s, down, rows, 0, SEND_DN, RECV_DN).wait_recv()
@@ -368,12 +380,8 @@
 
     lax.fori_loop(0, 3, stage, 0)
 
-    stores = [
-        pltpu.make_async_copy(buf.at[3, f, pl.ds(1, rows)], out.at[ORDER[f]], sems.at[LOAD, 2])
-        for f in range(5)
-    ]
-    for copy in stores:
-        copy.start()
+    for f in (U, PR, V):
+        store(f).start()
 
     def finish(s, carry):
         row_sends(s, up, 1, rows + 1, SEND_UP, RECV_UP).wait_send()
@@ -387,7 +395,7 @@
         def _():
             done(col.at[s, 1], sems.at[SEND_R, s])
 
-        for half in range(2):
+        for half in range(1):
             @pl.when(on_edge)
             def _():
                 done(col.at[s, 0], sems.at[ONE_C + half, s])
@@ -403,7 +411,8 @@
         return carry
 
     lax.fori_loop(0, 3, finish, 0)
-    done(buf.at[3, :, pl.ds(1, rows)], sems.at[LOAD, 2])
+    done(buf.at[3, pl.ds(0, 3), pl.ds(1, rows)], sems.at[LOAD, 2])
+    done(buf.at[3, pl.ds(3, 2), pl.ds(1, rows)], sems.at[LOAD, 0])
 
 
 def on_device(n, t_count, state, speed, freq, adjacency):
@@ -426,12 +435,12 @@
             pltpu.VMEM((3, 2, cb, 8, levels), f32),
             pltpu.VMEM((3, 2, rb, 8, levels), f32),
             pltpu.VMEM((3, 48, 8, levels), f32),
-            pltpu.VMEM((3, 24, 8, levels), f32),
+            pltpu.VMEM((3, 48, 8, levels), f32),
             pltpu.VMEM((3, rb, 8, levels), f32),
             pltpu.VMEM((3, 2, cb, 8, levels), f32),
             pltpu.VMEM((3, 2, rb, 8, levels), f32),
             pltpu.VMEM((3, 2, cb, 2, 8, levels), f32),
-            pltpu.VMEM((3, 24, 8, levels), f32),
+            pltpu.VMEM((3, 48, 8, levels), f32),
             pltpu.VMEM((rows, cols, levels), f32),
             pltpu.VMEM((1, levels), f32),
             pltpu.VMEM((48, 8, levels), f32),

time: 42.9 us -> 42.6 us (level)
  no operation moved by 1% of the time
where the time goes in v3:
time: 42.6 us; the launch traced here: 42.4 us
  Pallas kernels  37.9 us (89%)
  local copies, waits for them, and re-layouts  4.48 us (11%)
    pallas_call x1, Pallas kernels, on_device(): pl.pallas_call(functools.partial(kernel, n, t_count, rows, cols, levels),...  37.9 us
    unnamed x2, local copies, waits for them, and re-layouts  3.87 us

profile of v3, /device:TPU:0, one launch (start us, length us, event | category | flops | bytes accessed | tf_op | source)
XLA Modules:
  0.0 42.4 jit_solution(17597275873860300632)
XLA Ops:
  0.0 0.8 %copy.6 = s32[6,4,3]{2,1,0:T(4,128)S(1)} copy(s32[6,4,3]{0,1,2:T(4,128)} %param.7) | data formatting | bytes 576 | tf_op args[3]
  0.8 0.6 %reshape.7.adj = s32[72]{0:T(128)} reshape(s32[6,4,3]{2,1,0:T(4,128)S(1)} %copy.6) | data formatting | bytes 576 | tf_op jit(solution)/shard_map/reshape | solution.py:452
  1.4 37.9 %shard_map.46 = f32[5,24,32,128]{3,2,1,0:T(8,128)} custom-call(f32[5,24,32,128]{3,2,1,0:T(8,128)} %state.1, f32[24,32,128]{2,1,0:T(8,128)} %speed.1, f32[1,128]{1,0:T(1,128)} %bitcast.1, s32[72]{0:T(128)} %reshape.7.adj), custom_call_target="tpu_custom_call" | custom-call | tf_op jit(solution)/shard_map/pallas_call | solution.py:422
  39.3 3.1 %copy.8 = f32[5,24,32,128]{3,2,1,0:T(8,128)} copy(f32[5,24,32,128]{3,2,1,0:T(8,128)} %shard_map.46) | data formatting | bytes 3932160

commit v4 on v3

--- a/solution.py
+++ b/solution.py
@@ -154,7 +154,6 @@
                     col[s, side, ib, 4 + t : 5 + t] = v * west_sign if side == 0 else v
             return carry
 
-        lax.fori_loop(0, row_blocks, pack_col, 0)
 
         @pl.when(has_start)
         def _():
@@ -186,6 +185,8 @@
                 return carry
 
             lax.fori_loop(0, col_blocks, one, 0)
+
+        lax.fori_loop(0, row_blocks, pack_col, 0)
 
         @pl.when(on_edge)
         def _():

time: 42.6 us -> 42.5 us (level)
  no operation moved by 1% of the time
where the time goes in v4:
time: 42.5 us; the launch traced here: 42.3 us
  Pallas kernels  37.8 us (89%)
  local copies, waits for them, and re-layouts  4.48 us (11%)
    pallas_call x1, Pallas kernels, on_device(): pl.pallas_call(functools.partial(kernel, n, t_count, rows, cols, levels),...  37.8 us
    unnamed x2, local copies, waits for them, and re-layouts  3.87 us

profile of v4, /device:TPU:0, one launch (start us, length us, event | category | flops | bytes accessed | tf_op | source)
XLA Modules:
  0.0 42.3 jit_solution(1179696179254681171)
XLA Ops:
  0.0 0.8 %copy.6 = s32[6,4,3]{2,1,0:T(4,128)S(1)} copy(s32[6,4,3]{0,1,2:T(4,128)} %param.7) | data formatting | bytes 576 | tf_op args[3]
  0.8 0.6 %reshape.7.adj = s32[72]{0:T(128)} reshape(s32[6,4,3]{2,1,0:T(4,128)S(1)} %copy.6) | data formatting | bytes 576 | tf_op jit(solution)/shard_map/reshape | solution.py:453
  1.4 37.8 %shard_map.46 = f32[5,24,32,128]{3,2,1,0:T(8,128)} custom-call(f32[5,24,32,128]{3,2,1,0:T(8,128)} %state.1, f32[24,32,128]{2,1,0:T(8,128)} %speed.1, f32[1,128]{1,0:T(1,128)} %bitcast.1, s32[72]{0:T(128)} %reshape.7.adj), custom_call_target="tpu_custom_call" | custom-call | tf_op jit(solution)/shard_map/pallas_call | solution.py:423
  39.2 3.1 %copy.8 = f32[5,24,32,128]{3,2,1,0:T(8,128)} copy(f32[5,24,32,128]{3,2,1,0:T(8,128)} %shard_map.46) | data formatting | bytes 3932160
